TPU v7x, 32 devices: a whole 2x2x4 slice. The times are simulated.
32 devices in a mesh: cfg: 1, pair: 16 (over z, y, x), blk: 2 (over core).
Axes of the slice: x: 2, y: 2, z: 4, core: 2. Of those that a mesh axis runs over, the one named last changes fastest.
Arguments:
- elementals: bfloat16 [16, 8, 2, 65536], P('cfg', None, None, ('pair', 'blk')), may hold values from -0.079589844 to 0.079589844
- perambulator: bfloat16 [16, 2, 1024, 1024], P(('cfg', 'pair'), None, None, 'blk'), may hold values from -0.1875 to 0.1875
- pairs: int32 [16, 2], replicated, may hold values from 0 to 15, as said below
- elem_index: int32 [16, 24], replicated, may hold values from 0 to 7
- coef_code: int32 [16, 24, 4, 4], replicated, may hold values from -2 to 2
- term_count: int32 [16], replicated, may hold values from 12 to 24, as said below
Outputs:
- correlator: float32 [16, 2], P(('cfg', 'pair'))
Inputs may be any that keep to these rules, and one draw needn't show every extreme that they name: `pairs`: pair p + 8 lists the two timeslices of pair p in reverse order; the two timeslices of a pair differ. `term_count`: some pair uses all 24 terms.
All inputs are finite; a program needn't handle non-finite values.
Results may differ from a plain program's by a relative error of at most 0.0057.
Values may be sent and summed in bfloat16 or wider, within the bound.
No kernel may reach another device: no remote copies, remote signals or barrier semaphores. Data moves between devices by JAX's collectives and lax.ppermute only.
A program may use at most 64 MiB of HBM per device.

v0:
```python
import jax
import jax.numpy as jnp
from jax import lax
from jax.sharding import PartitionSpec as P

NV = 256
NS = 4


def partner(value, axis, apart):
    return lax.ppermute(value, axis, [(i, i ^ 1 << apart) for i in range(lax.axis_size(axis))])


def shards(elementals, perambulator, pairs, elem_index, coef_code, term_count):
    peers = lax.axis_size("pair")
    entries = elementals.shape[-1]
    nterms = elem_index.shape[1]
    used = (jnp.arange(nterms)[None, :] < term_count[:, None]).astype(jnp.float32)
    weights = (coef_code.astype(jnp.float32) * 0.5 * used[:, :, None, None]).astype(jnp.bfloat16)
    picked = elementals[pairs[:, 0][:, None], elem_index]
    combined = jnp.einsum(
        "pkab,pkcf->pabcf", weights, picked, preferred_element_type=jnp.float32
    ).astype(jnp.bfloat16)
    blocks = lax.all_to_all(combined, "pair", split_axis=0, concat_axis=0, tiled=True)
    gathered = lax.all_gather(blocks[:, None], "blk", axis=1, tiled=True)
    propagator = perambulator[0]
    columns = propagator.shape[-1]
    shaped = gathered.reshape(2 * peers, NS, NS, 2, entries // NV, NV)
    phi_real = shaped[:, :, :, 0]
    phi_imag = shaped[:, :, :, 1]
    prop_real = propagator[0].reshape(NS, NV, columns)
    prop_imag = propagator[1].reshape(NS, NV, columns)
    form = "gabuj,bjn->agun"
    dressed_real = jnp.einsum(
        form, phi_real, prop_real, preferred_element_type=jnp.float32
    ) - jnp.einsum(form, phi_imag, prop_imag, preferred_element_type=jnp.float32)
    dressed_imag = jnp.einsum(
        form, phi_real, prop_imag, preferred_element_type=jnp.float32
    ) + jnp.einsum(form, phi_imag, prop_real, preferred_element_type=jnp.float32)
    dressed = (
        jnp.stack([dressed_real, dressed_imag]).astype(jnp.bfloat16).reshape(2, NS * NV, columns)
    )
    mirror_bit = peers.bit_length() - 2
    mirror = partner(dressed, "pair", mirror_bit)
    mirror_rows = lax.all_to_all(mirror, "blk", split_axis=1, concat_axis=2, tiled=True)
    products = jnp.einsum("zrc,ycr->zy", dressed, mirror_rows, preferred_element_type=jnp.float32)
    partial_trace = jnp.stack([products[0, 0] - products[1, 1], products[0, 1] + products[1, 0]])
    total = lax.psum(partial_trace, "blk")
    return total[None, :]


def solution(mesh):
    return jax.shard_map(
        shards,
        mesh=mesh,
        in_specs=(
            P("cfg", None, None, ("pair", "blk")),
            P(("cfg", "pair"), None, None, "blk"),
            P(),
            P(),
            P(),
            P(),
        ),
        out_specs=P(("cfg", "pair"), None),
        check_vma=False,
    )
```

profile of v0, /device:TPU:0, one launch (start us, length us, event | category | flops | bytes accessed | tf_op | source)
XLA Modules:
  0.0 274.8 jit_solution(7903193112295483595)
XLA Ops:
  6.5 0.0 copy-start
  6.5 0.0 all-gather.3.cloned.1.call-start
  6.5 0.8 fusion.23
  7.3 0.8 fusion.19
  8.1 0.1 reshape.44
  8.2 0.7 fusion.20
  8.9 0.0 copy-done
  8.9 0.0 copy-start.6
  8.9 19.0 %gather_fusion = bf16[384,2,2048]{2,1,0:T(2,128)(2,1)} fusion(bf16[16,8,2,2048]{3,2,1,0:T(2,128)(2,1)S(1)} %copy-done, s32[384]{0:T(512)S(1)} %reshape.44), kind=kCustom, calls=%fused_computation | custom fusion | bytes 6294528 | tf_op jit(solution)/shard_map/gather | solution.py:20
  28.0 0.0 copy-done.6
  28.0 4.5 %fusion.2 = bf16[16,4,4,2,2048]{4,2,3,1,0:T(4,128)(2,1)S(1)} fusion(bf16[16,24,2,2048,1]{3,2,1,0,4:T(2,128)(2,1)} %bitcast.96, s32[16,24,4,4]{1,3,2,0:T(4,128)S(1)} %copy-done.6, f32[16,24]{1,0:T(8,128)S(1)} %fusion.20), kind=kOutput, calls=%fused_computation.3 | convolution fusion | flops 51398656 | bytes 5268992 | tf_op jit(solution)/shard_map/pkab,pkcf->pabcf/dot_general | solution.py:21
  32.5 57.0 %all_to_all.23 = bf16[16,4,4,2,2048]{4,2,3,1,0:T(4,128)(2,1)} all-to-all(bf16[16,4,4,2,2048]{4,2,3,1,0:T(4,128)(2,1)S(1)} %fusion.2), channel_id=1, replica_groups=mesh['cfg'=1,'pair'=16,'blk'=2] {'pair'}, dimensions={0} | all-to-all | bytes 4194304 | tf_op jit(solution)/shard_map/all_to_all | solution.py:24
  89.5 0.0 copy-start.3
  89.5 0.0 all-gather.3.cloned.1.call-update
  89.5 1.6 copy-done.3
  91.1 1.5 fusion.24
  92.6 0.0 copy-start.4
  92.6 9.1 %all-gather.3.cloned.1.call-done = bf16[16,8,4,2,2048]{4,2,3,1,0:T(4,128)(2,1)} async-done(((bf16[16,4,4,2,2048]{4,2,3,1,0:T(4,128)(2,1)}), bf16[16,8,4,2,2048]{4,2,3,1,0:T(4,128)(2,1)}) %all-gather.3.cloned.1.call-update) | async-done | bytes 4194320 | tf_op jit(solution)/shard_map/all_gather | solution.py:25
  101.7 7.7 %reshape.43 = bf16[32,4,4,2,8,256]{5,4,2,3,1,0:T(8,128)(2,1)} reshape(bf16[16,8,4,2,2048]{4,2,3,1,0:T(4,128)(2,1)} %all-gather.3.cloned.1.call-done) | data formatting | bytes 8388608 | tf_op jit(solution)/shard_map/reshape | solution.py:28
  109.4 0.0 copy-done.4
  109.4 0.0 copy-start.1
  109.4 0.0 copy-start.5
  109.4 3.0 %fusion.7 = f32[32,4,8,512,1]{3,2,4,1,0:T(8,128)S(1)} fusion(bf16[4,256,512,1,1]{2,1,0,4,3:T(8,128)(2,1)S(1)} %bitcast.102, bf16[32,4,4,2,8,256]{5,4,2,3,1,0:T(8,128)(2,1)} %reshape.43), kind=kOutput, calls=%fused_computation.12 | convolution fusion | flops 1073741824 | bytes 5242880 | tf_op jit(solution)/shard_map/gabuj,bjn->agun/dot_general | solution.py:37
  112.4 0.0 copy-done.1
  112.4 0.1 copy-done.5
  112.5 2.6 fusion.8
  115.1 1.3 fusion.12
  116.3 1.1 copy.32
  117.4 4.7 %copy.34 = bf16[1,1024,512]{1,0,2:T(2,128)(2,1)S(1)} copy(bf16[1,1024,512]{2,1,0:T(8,128)(2,1)} %bitcast.99) | data formatting | bytes 2097152 | tf_op jit(solution)/shard_map/stack | solution.py:41
  122.2 3.8 %fusion.11 = bf16[4,32,8,512]{3,2,0,1:T(8,128)(2,1)S(1)} fusion(bf16[4,256,512,1,1]{2,1,0,4,3:T(8,128)(2,1)} %bitcast.101, bf16[32,4,4,2,8,256]{5,4,2,3,1,0:T(8,128)(2,1)} %reshape.43, f32[32,4,8,512,1]{3,2,4,1,0:T(8,128)} %fusion.8), kind=kOutput, calls=%fused_computation.16 | convolution fusion | flops 1074790400 | bytes 6291456 | tf_op jit(solution)/shard_map/gabuj,bjn->agun/dot_general | solution.py:36
  126.0 1.1 copy.31
  127.1 6.0 %copy.33 = bf16[1,1024,512]{1,0,2:T(2,128)(2,1)} copy(bf16[1,1024,512]{2,1,0:T(8,128)(2,1)} %bitcast.100) | data formatting | bytes 2097152 | tf_op jit(solution)/shard_map/stack | solution.py:41
  133.0 5.9 %pad_maximum_fusion = bf16[2,1024,512]{1,0,2:T(2,128)(2,1)S(1)} fusion(bf16[1,1024,512]{1,0,2:T(2,128)(2,1)S(1)} %copy.34, bf16[1,1024,512]{1,0,2:T(2,128)(2,1)} %copy.33), kind=kLoop, calls=%fused_computation.6 | loop fusion | flops 4194304 | bytes 4194304 | tf_op jit(solution)/shard_map/stack | solution.py:41
  138.9 0.0 copy-start.2
  138.9 2.7 collective-permute-start
  141.7 0.0 copy-done.2
  141.7 91.1 %collective-permute-done = bf16[2,1024,512]{1,0,2:T(2,128)(2,1)} collective-permute-done((bf16[2,1024,512]{1,0,2:T(2,128)(2,1)S(1)}, bf16[2,1024,512]{1,0,2:T(2,128)(2,1)}, u32[]{:S(2)}, u32[]{:S(2)}) %collective-permute-start) | collective-permute-done | bytes 2097184 | tf_op jit(solution)/shard_map/ppermute | solution.py:11
  232.8 8.3 %copy.35 = bf16[2,1024,512]{2,0,1:T(2,128)(2,1)S(1)} copy(bf16[2,1024,512]{1,0,2:T(2,128)(2,1)} %collective-permute-done) | data formatting | bytes 4194304 | tf_op jit(solution)/shard_map/ppermute | solution.py:11
  241.1 5.4 %all_to_all.24 = bf16[2,1024,512]{2,0,1:T(2,128)(2,1)S(1)} all-to-all(bf16[2,1024,512]{2,0,1:T(2,128)(2,1)S(1)} %copy.35), channel_id=1, replica_groups=mesh['cfg'=1,'pair'=16,'blk'=2] {'blk'}, dimensions={1} | all-to-all | bytes 4194304 | tf_op jit(solution)/shard_map/all_to_all | solution.py:45
  246.5 3.2 %copy.54 = bf16[2,2,512,512]{3,1,0,2:T(2,128)(2,1)S(1)} copy(bf16[2,2,512,512]{3,0,2,1:T(2,128)(2,1)S(1)} %bitcast.97) | data formatting | bytes 4194304 | tf_op jit(solution)/shard_map/all_to_all | solution.py:45
  249.8 2.6 all_to_all.20
  252.4 9.3 %convolution_bitcast_fusion = f32[2,2]{1,0:T(2,128)S(1)} fusion(bf16[2,1024,512]{1,0,2:T(2,128)(2,1)} %copy-done.2, bf16[2,512,1024]{2,0,1:T(2,128)(2,1)} %all_to_all.20), kind=kOutput, calls=%fused_computation.18 | convolution fusion | flops 4194304 | bytes 4194320 | tf_op jit(solution)/shard_map/zrc,ycr->zy/dot_general | solution.py:46
  261.7 0.7 fusion.25
  264.9 0.1 maximum_bitcast_fusion
  265.0 2.9 %psum.7 = f32[1,2]{1,0:T(1,128)} all-reduce(f32[1,2]{1,0:T(1,128)S(1)} %maximum_bitcast_fusion), channel_id=1, replica_groups=mesh['cfg'=1,'pair'=16,'blk'=2] {'blk'}, use_global_device_ids=true, to_apply=%region_0.0 | all-reduce | flops 2 | bytes 16 | tf_op jit(solution)/shard_map/psum | solution.py:48
Async XLA Ops:
  6.5 2.4 copy-start
  6.5 95.2 %all-gather.3.cloned.1.call-start = ((), (), s32[]{:S(2)}) async-start(), calls=%async_computation.2 | async-start | bytes 6291456 | tf_op jit(solution)/shard_map/all_gather | solution.py:25
  8.9 19.1 %copy-start.6 = (s32[16,24,4,4]{1,3,2,0:T(4,128)S(1)}, s32[16,24,4,4]{1,3,2,0:T(4,128)}, u32[]{:S(2)}) copy-start(s32[16,24,4,4]{1,3,2,0:T(4,128)} %param.10) | copy-start | bytes 73732
  89.5 1.6 copy-start.3
  92.6 16.8 %copy-start.4 = (bf16[1,1,1024,512]{3,2,1,0:T(8,128)(2,1)S(1)}, bf16[1,1,1024,512]{3,2,1,0:T(8,128)(2,1)}, u32[]{:S(2)}) copy-start(bf16[1,1,1024,512]{3,2,1,0:T(8,128)(2,1)} %get-tuple-element.5) | copy-start | bytes 3145732
  109.4 3.0 %copy-start.1 = (bf16[32,4,4,2,8,256]{5,4,2,3,1,0:T(8,128)(2,1)S(1)}, bf16[32,4,4,2,8,256]{5,4,2,3,1,0:T(8,128)(2,1)}, u32[]{:S(2)}) copy-start(bf16[32,4,4,2,8,256]{5,4,2,3,1,0:T(8,128)(2,1)} %reshape.43) | copy-start | bytes 12582916
  109.4 3.1 %copy-start.5 = (bf16[1,1,1024,512]{3,2,1,0:T(8,128)(2,1)S(1)}, bf16[1,1,1024,512]{3,2,1,0:T(8,128)(2,1)}, u32[]{:S(2)}) copy-start(bf16[1,1,1024,512]{3,2,1,0:T(8,128)(2,1)} %get-tuple-element.6) | copy-start | bytes 3145732
  138.9 2.8 %copy-start.2 = (bf16[2,1024,512]{1,0,2:T(2,128)(2,1)}, bf16[2,1024,512]{1,0,2:T(2,128)(2,1)S(1)}, u32[]{:S(2)}) copy-start(bf16[2,1024,512]{1,0,2:T(2,128)(2,1)S(1)} %pad_maximum_fusion) | copy-start | bytes 6291460
  138.9 93.9 %collective-permute-start = (bf16[2,1024,512]{1,0,2:T(2,128)(2,1)S(1)}, bf16[2,1024,512]{1,0,2:T(2,128)(2,1)}, u32[]{:S(2)}, u32[]{:S(2)}) collective-permute-start(bf16[2,1024,512]{1,0,2:T(2,128)(2,1)S(1)} %pad_maximum_fusion), channel_id=1, source_target_pairs={{0,16},{2,18},{4,20},{6,22},{8,24},{10,26},{12,28},{14,30},{16,0},... | collective-permute-start | bytes 6291464 | tf_op jit(solution)/shard_map/ppermute | solution.py:11
Sparse Core Ops, SparseCore 0:
  89.7 11.9 all-gather.2
where the time goes:
time: 276 us; the launch traced here: 275 us
  waiting for transfers between devices  100 us (36%)
  blocking collectives  65.4 us (24%)
  local copies, waits for them, and re-layouts  57.7 us (21%)
  matrix products  24.4 us (9%)
  between operations  16 us (6%)
  other arithmetic  8.21 us (3%)
    ppermute x1, waiting for transfers between devices, partner(): lax.ppermute(value, axis, [(i, i ^ 1 << apart) for i in range(lax.axis_si...  91.1 us
    all_to_all x1, blocking collectives, shards(): lax.all_to_all(combined, 'pair', split_axis=0, concat_axis=0, tiled=True)  57 us
    gather x1, local copies, waits for them, and re-layouts, shards(): picked = elementals[pairs[:, 0][:, None], elem_index]  19 us
    another operation x2, local copies, waits for them, and re-layouts, shards(): jnp.stack([dressed_real, dressed_imag]).astype(jnp.bfloat16)  10.7 us
    dot_general x1, matrix products, shards(): jnp.einsum('zrc,ycr->zy', dressed, mirror_rows, preferred_element_type=jn...  9.3 us
    all_gather x1, waiting for transfers between devices, shards(): gathered = lax.all_gather(blocks[:, None], 'blk', axis=1, tiled=True)  9.09 us
    ppermute x1, local copies, waits for them, and re-layouts, partner(): lax.ppermute(value, axis, [(i, i ^ 1 << apart) for i in range(lax.axis_si...  8.31 us
    reshape x1, local copies, waits for them, and re-layouts, shards(): shaped = gathered.reshape(2 * peers, NS, NS, 2, entries // NV, NV)  7.7 us
  transfers between devices with their start and end apart: 2, of which 2 were waited for; matrix products, arithmetic and copies ran while one was open for 1% of the time, Pallas kernels for 0%

commit v1 on v0

--- a/solution.py
+++ b/solution.py
@@ -42,7 +42,10 @@
     )
     mirror_bit = peers.bit_length() - 2
     mirror = partner(dressed, "pair", mirror_bit)
-    mirror_rows = lax.all_to_all(mirror, "blk", split_axis=1, concat_axis=2, tiled=True)
+    mirror_rows = jnp.concatenate(
+        lax.all_to_all(jnp.stack(jnp.split(mirror, lax.axis_size("blk"), axis=1)), "blk", 0, 0),
+        axis=2,
+    )
     products = jnp.einsum("zrc,ycr->zy", dressed, mirror_rows, preferred_element_type=jnp.float32)
     partial_trace = jnp.stack([products[0, 0] - products[1, 1], products[0, 1] + products[1, 0]])
     total = lax.psum(partial_trace, "blk")

time: 276 us -> 272 us (0.986)
  local copies, waits for them, and re-layouts: 57.7 us -> 51.6 us
  other arithmetic: 8.21 us -> 11.2 us
    ppermute x1 -> x0, local copies, waits for them, and re-layouts: 8.31 us -> none  [partner(): lax.ppermute(value, axis, [(i, i ^ 1 << apart) for i in range(lax.axis_si...]
    reshape x0 -> x1, local copies, waits for them, and re-layouts: none -> 6.6 us  [shards(): jnp.concatenate(lax.all_to_all(jnp.stack(jnp.split(mirror, lax.axis_size(...]
    all_to_all x2 -> x0, local copies, waits for them, and re-layouts: 5.85 us -> none  [shards(): lax.all_to_all(mirror, 'blk', split_axis=1, concat_axis=2, tiled=True)]
    another operation x0 -> x1, other arithmetic: none -> 2.96 us  [shards(): jnp.stack(jnp.split(mirror, lax.axis_size('blk'), axis=1))]
where the time goes in v1:
time: 272 us; the launch traced here: 271 us
  waiting for transfers between devices  100 us (37%)
  blocking collectives  65.4 us (24%)
  local copies, waits for them, and re-layouts  51.6 us (19%)
  matrix products  24.4 us (9%)
  between operations  16 us (6%)
  other arithmetic  11.2 us (4%)
  starting transfers between devices  2.74 us (1%)
    ppermute x1, waiting for transfers between devices, partner(): lax.ppermute(value, axis, [(i, i ^ 1 << apart) for i in range(lax.axis_si...  91 us
    all_to_all x1, blocking collectives, shards(): lax.all_to_all(combined, 'pair', split_axis=0, concat_axis=0, tiled=True)  57 us
    gather x1, local copies, waits for them, and re-layouts, shards(): picked = elementals[pairs[:, 0][:, None], elem_index]  19 us
    another operation x2, local copies, waits for them, and re-layouts, shards(): jnp.stack([dressed_real, dressed_imag]).astype(jnp.bfloat16)  10.7 us
    dot_general x1, matrix products, shards(): jnp.einsum('zrc,ycr->zy', dressed, mirror_rows, preferred_element_type=jn...  9.3 us
    all_gather x1, waiting for transfers between devices, shards(): gathered = lax.all_gather(blocks[:, None], 'blk', axis=1, tiled=True)  9.08 us
    reshape x1, local copies, waits for them, and re-layouts, shards(): shaped = gathered.reshape(2 * peers, NS, NS, 2, entries // NV, NV)  7.7 us
    reshape x1, local copies, waits for them, and re-layouts, shards(): jnp.concatenate(lax.all_to_all(jnp.stack(jnp.split(mirror, lax.axis_size(...  6.6 us
  transfers between devices with their start and end apart: 2, of which 2 were waited for; matrix products, arithmetic and copies ran while one was open for 1% of the time, Pallas kernels for 0%

profile of v1, /device:TPU:0, one launch (start us, length us, event | category | flops | bytes accessed | tf_op | source)
XLA Modules:
  0.0 271.4 jit_solution(1013394576069577573)
XLA Ops:
  6.5 0.0 copy-start
  6.5 0.0 all-gather.3.cloned.1.call-start
  6.5 0.8 fusion.23
  7.3 0.8 fusion.19
  8.1 0.1 reshape.52
  8.2 0.7 fusion.20
  8.9 0.0 copy-done
  8.9 0.0 copy-start.6
  8.9 19.0 %gather_fusion = bf16[384,2,2048]{2,1,0:T(2,128)(2,1)} fusion(bf16[16,8,2,2048]{3,2,1,0:T(2,128)(2,1)S(1)} %copy-done, s32[384]{0:T(512)S(1)} %reshape.52), kind=kCustom, calls=%fused_computation | custom fusion | bytes 6294528 | tf_op jit(solution)/shard_map/gather | solution.py:20
  28.0 0.0 copy-done.6
  28.0 4.5 %fusion.2 = bf16[16,4,4,2,2048]{4,2,3,1,0:T(4,128)(2,1)S(1)} fusion(bf16[16,24,2,2048,1]{3,2,1,0,4:T(2,128)(2,1)} %bitcast.97, s32[16,24,4,4]{1,3,2,0:T(4,128)S(1)} %copy-done.6, f32[16,24]{1,0:T(8,128)S(1)} %fusion.20), kind=kOutput, calls=%fused_computation.3 | convolution fusion | flops 51398656 | bytes 5268992 | tf_op jit(solution)/shard_map/pkab,pkcf->pabcf/dot_general | solution.py:21
  32.5 57.0 %all_to_all.10 = bf16[16,4,4,2,2048]{4,2,3,1,0:T(4,128)(2,1)} all-to-all(bf16[16,4,4,2,2048]{4,2,3,1,0:T(4,128)(2,1)S(1)} %fusion.2), channel_id=1, replica_groups=mesh['cfg'=1,'pair'=16,'blk'=2] {'pair'}, dimensions={0} | all-to-all | bytes 4194304 | tf_op jit(solution)/shard_map/all_to_all | solution.py:24
  89.5 0.0 copy-start.3
  89.5 0.0 all-gather.3.cloned.1.call-update
  89.5 1.6 copy-done.3
  91.1 1.5 fusion.24
  92.6 0.0 copy-start.4
  92.6 9.1 %all-gather.3.cloned.1.call-done = bf16[16,8,4,2,2048]{4,2,3,1,0:T(4,128)(2,1)} async-done(((bf16[16,4,4,2,2048]{4,2,3,1,0:T(4,128)(2,1)}), bf16[16,8,4,2,2048]{4,2,3,1,0:T(4,128)(2,1)}) %all-gather.3.cloned.1.call-update) | async-done | bytes 4194320 | tf_op jit(solution)/shard_map/all_gather | solution.py:25
  101.7 7.7 %reshape.49 = bf16[32,4,4,2,8,256]{5,4,2,3,1,0:T(8,128)(2,1)} reshape(bf16[16,8,4,2,2048]{4,2,3,1,0:T(4,128)(2,1)} %all-gather.3.cloned.1.call-done) | data formatting | bytes 8388608 | tf_op jit(solution)/shard_map/reshape | solution.py:28
  109.4 0.0 copy-done.4
  109.4 0.0 copy-start.1
  109.4 0.0 copy-start.5
  109.4 3.0 %fusion.7 = f32[32,4,8,512,1]{3,2,4,1,0:T(8,128)S(1)} fusion(bf16[4,256,512,1,1]{2,1,0,4,3:T(8,128)(2,1)S(1)} %bitcast.102, bf16[32,4,4,2,8,256]{5,4,2,3,1,0:T(8,128)(2,1)} %reshape.49), kind=kOutput, calls=%fused_computation.12 | convolution fusion | flops 1073741824 | bytes 5242880 | tf_op jit(solution)/shard_map/gabuj,bjn->agun/dot_general | solution.py:37
  112.4 0.0 copy-done.1
  112.4 0.1 copy-done.5
  112.5 2.6 fusion.8
  115.1 1.2 fusion.12
  116.3 1.1 copy.15
  117.4 4.7 %copy.17 = bf16[1,1024,512]{1,0,2:T(2,128)(2,1)S(1)} copy(bf16[1,1024,512]{2,1,0:T(8,128)(2,1)} %bitcast.99) | data formatting | bytes 2097152 | tf_op jit(solution)/shard_map/stack | solution.py:41
  122.2 3.8 %fusion.11 = bf16[4,32,8,512]{3,2,0,1:T(8,128)(2,1)S(1)} fusion(bf16[4,256,512,1,1]{2,1,0,4,3:T(8,128)(2,1)} %bitcast.101, bf16[32,4,4,2,8,256]{5,4,2,3,1,0:T(8,128)(2,1)} %reshape.49, f32[32,4,8,512,1]{3,2,4,1,0:T(8,128)} %fusion.8), kind=kOutput, calls=%fused_computation.16 | convolution fusion | flops 1074790400 | bytes 6291456 | tf_op jit(solution)/shard_map/gabuj,bjn->agun/dot_general | solution.py:36
  126.0 1.1 copy.14
  127.0 6.0 %copy.16 = bf16[1,1024,512]{1,0,2:T(2,128)(2,1)} copy(bf16[1,1024,512]{2,1,0:T(8,128)(2,1)} %bitcast.100) | data formatting | bytes 2097152 | tf_op jit(solution)/shard_map/stack | solution.py:41
  133.0 5.9 %pad_maximum_fusion = bf16[2,1024,512]{1,0,2:T(2,128)(2,1)S(1)} fusion(bf16[1,1024,512]{1,0,2:T(2,128)(2,1)S(1)} %copy.17, bf16[1,1024,512]{1,0,2:T(2,128)(2,1)} %copy.16), kind=kLoop, calls=%fused_computation.6 | loop fusion | flops 4194304 | bytes 4194304 | tf_op jit(solution)/shard_map/stack | solution.py:41
  138.9 0.0 copy-start.2
  138.9 2.7 %collective-permute-start = (bf16[2,1024,512]{1,0,2:T(2,128)(2,1)S(1)}, bf16[2,1024,512]{1,0,2:T(2,128)(2,1)S(1)}, u32[]{:S(2)}, u32[]{:S(2)}) collective-permute-start(bf16[2,1024,512]{1,0,2:T(2,128)(2,1)S(1)} %pad_maximum_fusion), channel_id=1, source_target_pairs={{0,16},{2,18},{4,20},{6,22},{8,24},{10,26},{12,28},{14,30},{16,0},... | collective-permute-start | bytes 6291464 | tf_op jit(solution)/shard_map/ppermute | solution.py:11
  141.7 0.0 copy-done.2
  141.7 91.0 %collective-permute-done = bf16[2,1024,512]{1,0,2:T(2,128)(2,1)S(1)} collective-permute-done((bf16[2,1024,512]{1,0,2:T(2,128)(2,1)S(1)}, bf16[2,1024,512]{1,0,2:T(2,128)(2,1)S(1)}, u32[]{:S(2)}, u32[]{:S(2)}) %collective-permute-start) | collective-permute-done | bytes 2097184 | tf_op jit(solution)/shard_map/ppermute | solution.py:11
  232.7 1.5 slice_bitcast_fusion.15
  234.1 3.0 %pad_maximum_fusion.1 = bf16[2,2,512,512]{2,1,3,0:T(2,128)(2,1)S(1)} fusion(bf16[1,2,512,512]{2,1,3,0:T(2,128)(2,1)S(1)} %get-tuple-element.6, bf16[1,2,512,512]{2,1,3,0:T(2,128)(2,1)S(1)} %get-tuple-element.5), kind=kLoop, calls=%fused_computation.7 | loop fusion | flops 1048576 | bytes 4194304 | tf_op jit(solution)/shard_map/stack | solution.py:46
  237.1 5.4 %all_to_all.11 = bf16[2,2,512,512]{2,1,3,0:T(2,128)(2,1)S(1)} all-to-all(bf16[2,2,512,512]{2,1,3,0:T(2,128)(2,1)S(1)} %pad_maximum_fusion.1), channel_id=1, replica_groups=mesh['cfg'=1,'pair'=16,'blk'=2] {'blk'}, dimensions={0} | all-to-all | bytes 4194304 | tf_op jit(solution)/shard_map/all_to_all | solution.py:46
  242.5 6.6 %copy.29 = bf16[2,512,1024]{2,0,1:T(2,128)(2,1)} copy(bf16[2,512,1024]{1,0,2:T(2,128)(2,1)S(1)} %bitcast.98) | data formatting | bytes 4194304 | tf_op jit(solution)/shard_map/reshape | solution.py:45
  249.1 9.3 %convolution_bitcast_fusion = f32[2,2]{1,0:T(2,128)S(1)} fusion(bf16[2,1024,512]{1,0,2:T(2,128)(2,1)} %copy-done.2, bf16[2,512,1024]{2,0,1:T(2,128)(2,1)} %copy.29), kind=kOutput, calls=%fused_computation.18 | convolution fusion | flops 4194304 | bytes 4194320 | tf_op jit(solution)/shard_map/zrc,ycr->zy/dot_general | solution.py:49
  258.4 0.6 fusion.25
  261.5 0.1 maximum_bitcast_fusion
  261.6 2.9 %psum.7 = f32[1,2]{1,0:T(1,128)} all-reduce(f32[1,2]{1,0:T(1,128)S(1)} %maximum_bitcast_fusion), channel_id=1, replica_groups=mesh['cfg'=1,'pair'=16,'blk'=2] {'blk'}, use_global_device_ids=true, to_apply=%region_0.0 | all-reduce | flops 2 | bytes 16 | tf_op jit(solution)/shard_map/psum | solution.py:51
Async XLA Ops:
  6.5 2.4 copy-start
  6.5 95.2 %all-gather.3.cloned.1.call-start = ((), (), s32[]{:S(2)}) async-start(), calls=%async_computation.2 | async-start | bytes 6291456 | tf_op jit(solution)/shard_map/all_gather | solution.py:25
  8.9 19.1 %copy-start.6 = (s32[16,24,4,4]{1,3,2,0:T(4,128)S(1)}, s32[16,24,4,4]{1,3,2,0:T(4,128)}, u32[]{:S(2)}) copy-start(s32[16,24,4,4]{1,3,2,0:T(4,128)} %param.10) | copy-start | bytes 73732
  89.5 1.6 copy-start.3
  92.6 16.8 %copy-start.4 = (bf16[1,1,1024,512]{3,2,1,0:T(8,128)(2,1)S(1)}, bf16[1,1,1024,512]{3,2,1,0:T(8,128)(2,1)}, u32[]{:S(2)}) copy-start(bf16[1,1,1024,512]{3,2,1,0:T(8,128)(2,1)} %get-tuple-element.7) | copy-start | bytes 3145732
  109.4 3.0 %copy-start.1 = (bf16[32,4,4,2,8,256]{5,4,2,3,1,0:T(8,128)(2,1)S(1)}, bf16[32,4,4,2,8,256]{5,4,2,3,1,0:T(8,128)(2,1)}, u32[]{:S(2)}) copy-start(bf16[32,4,4,2,8,256]{5,4,2,3,1,0:T(8,128)(2,1)} %reshape.49) | copy-start | bytes 12582916
  109.4 3.1 %copy-start.5 = (bf16[1,1,1024,512]{3,2,1,0:T(8,128)(2,1)S(1)}, bf16[1,1,1024,512]{3,2,1,0:T(8,128)(2,1)}, u32[]{:S(2)}) copy-start(bf16[1,1,1024,512]{3,2,1,0:T(8,128)(2,1)} %get-tuple-element.8) | copy-start | bytes 3145732
  138.9 2.8 %copy-start.2 = (bf16[2,1024,512]{1,0,2:T(2,128)(2,1)}, bf16[2,1024,512]{1,0,2:T(2,128)(2,1)S(1)}, u32[]{:S(2)}) copy-start(bf16[2,1024,512]{1,0,2:T(2,128)(2,1)S(1)} %pad_maximum_fusion) | copy-start | bytes 6291460
  138.9 93.8 %collective-permute-start = (bf16[2,1024,512]{1,0,2:T(2,128)(2,1)S(1)}, bf16[2,1024,512]{1,0,2:T(2,128)(2,1)S(1)}, u32[]{:S(2)}, u32[]{:S(2)}) collective-permute-start(bf16[2,1024,512]{1,0,2:T(2,128)(2,1)S(1)} %pad_maximum_fusion), channel_id=1, source_target_pairs={{0,16},{2,18},{4,20},{6,22},{8,24},{10,26},{12,28},{14,30},{16,0},... | collective-permute-start | bytes 6291464 | tf_op jit(solution)/shard_map/ppermute | solution.py:11
Sparse Core Ops, SparseCore 0:
  89.7 11.9 all-gather.2
